TPU v7x, 32 devices: a whole 2x2x4 slice. The times are simulated.
32 devices in a mesh: parts: 2 (over x), row: 16 (over z, y, core).
Axes of the slice: x: 2, y: 2, z: 4, core: 2. Of those that a mesh axis runs over, the one named last changes fastest.
Arguments:
- tile_values: bfloat16 [2048, 128, 128], P(('parts', 'row')), parts along dimension 0, may hold values from -0.09375 to 0.09375
- tile_row: int32 [2048], P(('parts', 'row')), parts along dimension 0, may hold values from 0 to 1
- tile_col: int32 [2048], P(('parts', 'row')), parts along dimension 0, may hold values from 0 to 15
- primal_start: float32 [4096, 128], P(('parts', 'row')), parts along dimension 0, may hold values from 0 to 1
- objective: float32 [4096, 128], P(('parts', 'row')), parts along dimension 0, may hold values from -3 to 3
- upper_bound: float32 [4096], P(('parts', 'row')), parts along dimension 0, may hold values from 0.3 to 3
- dual_start: float32 [8192, 128], P(('parts', 'row')), parts along dimension 0, may hold values from 0 to 1
- row_bound: float32 [8192, 128], P(('parts', 'row')), parts along dimension 0, may hold values from -6 to 6
Outputs:
- primal: float32 [4096, 128], P(('parts', 'row')), parts along dimension 0
- dual: float32 [8192, 128], P(('parts', 'row')), parts along dimension 0
There are 2 independent parts, one for each index of `parts`. A program takes and returns all parts, laid end to end along the dimension named above; each array names one. Nothing has to cross between parts.
All inputs are finite; a program needn't handle non-finite values.
Results may differ from a plain program's by a relative error of at most 0.0023.
Values may be sent and summed in bfloat16 or wider, within the bound.
A program may use at most 64 MiB of HBM per device.

v0:
```python
import functools

import jax
import jax.numpy as jnp
from jax import lax
from jax.experimental import pallas as pl
from jax.experimental.pallas import tpu as pltpu
from jax.sharding import PartitionSpec as P

ITERS = 3
HALVES = 2
STEP = 0.4
F32 = jnp.float32
BF16 = jnp.bfloat16


def dense_kernel(chunks, row_blocks, rows, cols, tiles, high, low, total, held, arrived):
    group = held.shape[0] // chunks

    def copy(k):
        part = pl.ds(k * group, group)
        return pltpu.make_async_copy(tiles.at[part], held.at[part], arrived.at[k])

    for k in range(chunks):
        copy(k).start()
    total[...] = jnp.zeros_like(total)
    for k in range(chunks):
        copy(k).wait()

        @pl.loop(0, group, unroll=min(group, 8))
        def _(i):
            t = k * group + i
            at = cols[t] * row_blocks + rows[t]
            total[at] += held[t].astype(F32)

    @pl.loop(0, total.shape[0], unroll=4)
    def _(b):
        value = total[b]
        rounded = value.astype(BF16)
        high[b] = rounded
        low[b] = (value - rounded.astype(F32)).astype(BF16)


def dense(tile_values, tile_row, tile_col, blocks, row_blocks):
    tiles, size, _ = tile_values.shape
    chunks = 8
    shape = jax.ShapeDtypeStruct((blocks * row_blocks, size, size), BF16)
    smem = pl.BlockSpec(memory_space=pltpu.SMEM)
    vmem = pl.BlockSpec(memory_space=pltpu.VMEM)
    room = size * size * (4 * blocks * row_blocks + 2 * tiles + 4 * blocks * row_blocks)
    return pl.pallas_call(
        functools.partial(dense_kernel, chunks, row_blocks),
        out_shape=(shape, shape),
        in_specs=[smem, smem, pl.BlockSpec(memory_space=pltpu.HBM)],
        out_specs=(vmem, vmem),
        scratch_shapes=[
            pltpu.VMEM((blocks * row_blocks, size, size), F32),
            pltpu.VMEM((tiles, size, size), BF16),
            pltpu.SemaphoreType.DMA((chunks,)),
        ],
        compiler_params=pltpu.CompilerParams(vmem_limit_bytes=room + (4 << 20)),
    )(tile_row, tile_col, tile_values)


def iterate_kernel(
    n, halves, high, low, primal_start, objective, upper, dual_start, row_bound,
    primal_out, dual_out,
    primal, dual, cost, bound, own, send1, recv1, send2, recv2, same, other,
    s1, r1, s2, r2, sx, rx, sf, rf,
):
    me = lax.axis_index("row")
    core = lax.rem(me, 2)
    chip = me // 2
    chips = n // 2
    partner = me + 1 - 2 * core
    size = primal.shape[1]
    part = primal.shape[0] // halves

    def peer(d):
        return lax.rem(chip + d, chips) * 2 + core

    def source(d):
        return lax.rem(chip + chips - d, chips) * 2

    def send(src, dst, send_sem, recv_sem, device):
        return pltpu.make_async_remote_copy(
            src_ref=src, dst_ref=dst, send_sem=send_sem, recv_sem=recv_sem,
            device_id={"row": device}, device_id_type=pl.DeviceIdType.MESH,
        )

    def to_partner(h, d):
        return send(send1.at[h, d], recv1.at[h, d], s1.at[h, d], r1.at[h, d], partner)

    def to_peer(h, d):
        return send(send2.at[h, d], recv2.at[h, d], s2.at[h, d], r2.at[h, d], peer(d))

    def spread(h, d):
        return send(same.at[h, 0], same.at[h, d], sx.at[h, d], rx.at[h, d], peer(d))

    def forward(h, d):
        return send(same.at[h, d], other.at[h, d], sf.at[h, d], rf.at[h, d], partner)

    order = list(range(1, chips)) + [0]

    def scenarios(h):
        return pl.ds(h * part, part)

    def partials(h, start):
        lowered = dual[scenarios(h), :].astype(BF16)
        for d in order:
            k = lax.rem(chip + d, chips)
            mine, theirs = 2 * k + core, 2 * k + 1 - core
            pair = jnp.dot(
                lowered, jnp.concatenate([high[theirs], high[mine]], axis=1),
                preferred_element_type=F32,
            ) + jnp.dot(
                lowered, jnp.concatenate([low[theirs], low[mine]], axis=1),
                preferred_element_type=F32,
            )
            send1[h, d] = pair[:, :size].astype(BF16)
            if start:
                to_partner(h, d).start()
            own[h, d] = pair[:, size:]

    def add_partner(h):
        for d in range(1, chips):
            to_partner(h, d).wait_recv()
            send2[h, d] = (own[h, d] + recv1[h, d].astype(F32)).astype(BF16)
            to_peer(h, d).start()

    def update(h):
        to_partner(h, 0).wait_recv()
        total = own[h, 0] + recv1[h, 0].astype(F32)
        for d in range(1, chips):
            to_peer(h, d).wait_recv()
            total += recv2[h, d].astype(F32)
        before = primal[scenarios(h), :]
        updated = jnp.clip(before - STEP * (cost[scenarios(h), :] - total), 0.0, upper[...])
        same[h, 0] = (2.0 * updated - before).astype(BF16)
        for d in range(1, chips):
            spread(h, d).start()
        forward(h, 0).start()
        primal[scenarios(h), :] = updated
        for d in range(chips):
            to_partner(h, d).wait_send()

    def pass_on(h):
        for d in range(1, chips):
            spread(h, d).wait_recv()
            forward(h, d).start()
        for d in range(1, chips):
            to_peer(h, d).wait_send()

    def image(h):
        total = jnp.zeros((part, dual.shape[1]), F32)
        for d in range(chips):
            forward(h, d).wait_recv()
            block = jnp.concatenate([same[h, d], other[h, d]], axis=1)
            a, b = source(d) + core, source(d) + 1 - core
            for ref in (high, low):
                total += lax.dot_general(
                    block, jnp.concatenate([ref[a], ref[b]], axis=1),
                    (((1,), (1,)), ((), ())), preferred_element_type=F32,
                )
        dual[scenarios(h), :] = jnp.maximum(
            dual[scenarios(h), :] + STEP * (bound[scenarios(h), :] - total), 0.0
        )
        for d in range(chips):
            forward(h, d).wait_send()
            if d:
                spread(h, d).wait_send()

    barrier = pltpu.get_barrier_semaphore()
    pl.semaphore_signal(
        barrier, inc=1, device_id={"row": partner}, device_id_type=pl.DeviceIdType.MESH
    )
    for d in range(1, chips):
        pl.semaphore_signal(
            barrier, inc=1, device_id={"row": peer(d)}, device_id_type=pl.DeviceIdType.MESH
        )
    dual[...] = dual_start[...].T
    for h in range(halves):
        partials(h, False)
    primal[...] = primal_start[...].T
    cost[...] = objective[...].T
    bound[...] = row_bound[...].T
    pl.semaphore_wait(barrier, chips)
    for h in range(halves):
        for d in order:
            to_partner(h, d).start()
    for h in range(halves):
        add_partner(h)

    def iteration(step, carry):
        more = step < ITERS - 1
        for h in range(halves):
            update(h)
        for h in range(halves):
            pass_on(h)
            if h:
                pl.when(more)(functools.partial(add_partner, h - 1))
            image(h)
            pl.when(more)(functools.partial(partials, h, True))
        pl.when(more)(functools.partial(add_partner, halves - 1))
        return carry

    lax.fori_loop(0, ITERS, iteration, 0)
    primal_out[...] = primal[...].T
    dual_out[...] = dual[...].T


def body(
    tile_values, tile_row, tile_col, primal_start, objective, upper_bound, dual_start, row_bound
):
    n = lax.axis_size("row")
    size = tile_values.shape[1]
    count = primal_start.shape[1]
    blocks = n * primal_start.shape[0] // size
    assert blocks == n and n % 2 == 0
    rows = dual_start.shape[0]
    row_blocks = rows // size
    high, low = dense(tile_values, tile_row, tile_col, blocks, row_blocks)
    chips = n // 2
    halves = HALVES
    part = count // halves
    vmem = pl.BlockSpec(memory_space=pltpu.VMEM)
    buffer = pltpu.VMEM((halves, chips, part, size), BF16)
    state = pltpu.VMEM((count, size), F32)
    long_state = pltpu.VMEM((count, rows), F32)
    room = 4 * blocks * rows * size + 16 * chips * count * size + (6 << 20)
    return pl.pallas_call(
        functools.partial(iterate_kernel, n, halves),
        out_shape=(
            jax.ShapeDtypeStruct(primal_start.shape, F32),
            jax.ShapeDtypeStruct(dual_start.shape, F32),
        ),
        in_specs=[vmem] * 7,
        out_specs=(vmem, vmem),
        scratch_shapes=[
            state, long_state, state, long_state,
            pltpu.VMEM((halves, chips, part, size), F32),
            buffer, buffer, buffer, buffer, buffer, buffer,
        ] + [pltpu.SemaphoreType.DMA((halves, chips))] * 8,
        compiler_params=pltpu.CompilerParams(
            collective_id=0, has_side_effects=True, vmem_limit_bytes=room
        ),
    )(
        high.reshape(blocks, rows, size), low.reshape(blocks, rows, size),
        primal_start, objective, upper_bound.reshape(1, -1), dual_start, row_bound,
    )


def solution(mesh):
    rows = P(("parts", "row"), None)
    flat = P(("parts", "row"))
    return jax.shard_map(
        body,
        mesh=mesh,
        in_specs=(P(("parts", "row"), None, None), flat, flat, rows, rows, flat, rows, rows),
        out_specs=(rows, rows),
        check_vma=False,
    )
```

profile of v0, /device:TPU:0, one launch (start us, length us, event | category | flops | bytes accessed | tf_op | source)
XLA Modules:
  0.0 63.7 jit_solution(6842049682817437384)
XLA Ops:
  0.6 0.0 copy-start.7
  0.6 0.0 copy-start
  0.7 1.6 %copy-done = bf16[64,128,128]{2,1,0:T(8,128)(2,1)S(1)} copy-done((bf16[64,128,128]{2,1,0:T(8,128)(2,1)S(1)}, bf16[64,128,128]{2,1,0:T(8,128)(2,1)}, u32[]{:S(2)}) %copy-start) | copy-done | bytes 2097176
  2.2 0.0 copy-start.5
  2.2 0.7 %copy-done.5 = s32[64]{0:T(128)S(1)} copy-done((s32[64]{0:T(128)S(1)}, s32[64]{0:T(128)}, u32[]{:S(2)}) %copy-start.5) | copy-done | bytes 280
  2.9 0.0 copy-start.6
  2.9 0.7 %copy-done.6 = s32[64]{0:T(128)S(1)} copy-done((s32[64]{0:T(128)S(1)}, s32[64]{0:T(128)}, u32[]{:S(2)}) %copy-start.6) | copy-done | bytes 280
  3.6 0.0 copy-start.1
  3.6 0.0 copy-start.2
  3.6 0.0 copy-start.3
  3.6 0.0 copy-start.4
  3.6 1.6 %shard_map.95 = (bf16[32,128,128]{2,1,0:T(8,128)(2,1)S(1)}, bf16[32,128,128]{2,1,0:T(8,128)(2,1)S(1)}) custom-call(s32[64]{0:T(128)S(1)} %copy-done.5, s32[64]{0:T(128)S(1)} %copy-done.6, bf16[64,128,128]{2,1,0:T(8,128)(2,1)S(1)} %copy-done), custom_call_target="tpu_custom_call" | custom-call | tf_op jit(solution)/shard_map/pallas_call | solution.py:51
  5.2 0.0 copy-done.7
  5.2 0.0 copy-done.1
  5.2 0.0 copy-done.2
  5.2 0.0 copy-done.3
  5.3 0.0 copy-done.4
  5.3 57.1 %shard_map.96 = (f32[128,128]{1,0:T(8,128)S(1)}, f32[256,128]{1,0:T(8,128)S(1)}) custom-call(bf16[16,256,128]{2,1,0:T(8,128)(2,1)S(1)} %bitcast.3, bf16[16,256,128]{2,1,0:T(8,128)(2,1)S(1)} %bitcast.4, f32[128,128]{1,0:T(8,128)S(1)} %copy-done.3, f32[128,128]{1,0:T(8,128)S(1)} %copy-done.4, f32[1,128]{1,0:T(1,128)S(1)} %bitcast.5, f32[256,128]{1,0:T(8,128)S(1)} %copy-done.1, ...), custom_call_target="tpu_custom_call" | custom-call | tf_op jit(solution)/shard_map/pallas_call | solution.py:231
  62.4 0.6 copy.12
  63.0 0.7 %copy.13 = f32[256,128]{1,0:T(8,128)} copy(f32[256,128]{1,0:T(8,128)S(1)} %get-tuple-element.9) | data formatting | bytes 262144
Async XLA Ops:
  0.6 4.6 %copy-start.7 = (f32[128]{0:T(128)S(1)}, f32[128]{0:T(128)}, u32[]{:S(2)}) copy-start(f32[128]{0:T(128)} %param.13) | copy-start | bytes 1540
  0.6 1.6 %copy-start = (bf16[64,128,128]{2,1,0:T(8,128)(2,1)S(1)}, bf16[64,128,128]{2,1,0:T(8,128)(2,1)}, u32[]{:S(2)}) copy-start(bf16[64,128,128]{2,1,0:T(8,128)(2,1)} %tiles.1) | copy-start | bytes 6291460
  2.2 0.7 %copy-start.5 = (s32[64]{0:T(128)S(1)}, s32[64]{0:T(128)}, u32[]{:S(2)}) copy-start(s32[64]{0:T(128)} %rows.1) | copy-start | bytes 772
  2.9 0.7 %copy-start.6 = (s32[64]{0:T(128)S(1)}, s32[64]{0:T(128)}, u32[]{:S(2)}) copy-start(s32[64]{0:T(128)} %cols.1) | copy-start | bytes 772
  3.6 1.7 %copy-start.1 = (f32[256,128]{1,0:T(8,128)S(1)}, f32[256,128]{1,0:T(8,128)}, u32[]{:S(2)}) copy-start(f32[256,128]{1,0:T(8,128)} %dual_start.1) | copy-start | bytes 393220
  3.6 1.7 %copy-start.2 = (f32[256,128]{1,0:T(8,128)S(1)}, f32[256,128]{1,0:T(8,128)}, u32[]{:S(2)}) copy-start(f32[256,128]{1,0:T(8,128)} %row_bound.1) | copy-start | bytes 393220
  3.6 1.7 %copy-start.3 = (f32[128,128]{1,0:T(8,128)S(1)}, f32[128,128]{1,0:T(8,128)}, u32[]{:S(2)}) copy-start(f32[128,128]{1,0:T(8,128)} %primal_start.1) | copy-start | bytes 196612
  3.6 1.7 %copy-start.4 = (f32[128,128]{1,0:T(8,128)S(1)}, f32[128,128]{1,0:T(8,128)}, u32[]{:S(2)}) copy-start(f32[128,128]{1,0:T(8,128)} %objective.1) | copy-start | bytes 196612
where the time goes:
time: 64.3 us; the launch traced here: 63.7 us
  Pallas kernels  58.8 us (91%)
  local copies, waits for them, and re-layouts  4.21 us (7%)
  between operations  0.71 us (1%)
    pallas_call x1, Pallas kernels, body(): pl.pallas_call(functools.partial(iterate_kernel, n, halves), out_shape=(j...  57.1 us
    unnamed x18, local copies, waits for them, and re-layouts  4.21 us
    pallas_call x1, Pallas kernels, dense(): pl.pallas_call(functools.partial(dense_kernel, chunks, row_blocks), out_s...  1.65 us

commit v1 on v0

--- a/solution.py
+++ b/solution.py
@@ -105,22 +105,31 @@
     def scenarios(h):
         return pl.ds(h * part, part)
 
+    def wide(left, blocks, axis):
+        total = None
+        for ref in (high, low):
+            right = jnp.concatenate([ref[c] for c in blocks], axis=1)
+            value = lax.dot_general(
+                left, right, (((1,), (axis,)), ((), ())), preferred_element_type=F32
+            )
+            total = value if total is None else total + value
+        return total
+
     def partials(h, start):
         lowered = dual[scenarios(h), :].astype(BF16)
-        for d in order:
-            k = lax.rem(chip + d, chips)
-            mine, theirs = 2 * k + core, 2 * k + 1 - core
-            pair = jnp.dot(
-                lowered, jnp.concatenate([high[theirs], high[mine]], axis=1),
-                preferred_element_type=F32,
-            ) + jnp.dot(
-                lowered, jnp.concatenate([low[theirs], low[mine]], axis=1),
-                preferred_element_type=F32,
-            )
-            send1[h, d] = pair[:, :size].astype(BF16)
-            if start:
-                to_partner(h, d).start()
-            own[h, d] = pair[:, size:]
+        for own_side in (False, True):
+            for i in range(0, chips, 2):
+                pair = order[i : i + 2]
+                side = core if own_side else 1 - core
+                value = wide(lowered, [lax.rem(chip + d, chips) * 2 + side for d in pair], 0)
+                for j, d in enumerate(pair):
+                    piece = value[:, j * size : (j + 1) * size]
+                    if own_side:
+                        own[h, d] = piece
+                    else:
+                        send1[h, d] = piece.astype(BF16)
+                        if start:
+                            to_partner(h, d).start()
 
     def add_partner(h):
         for d in range(1, chips):
@@ -152,16 +161,16 @@
             to_peer(h, d).wait_send()
 
     def image(h):
-        total = jnp.zeros((part, dual.shape[1]), F32)
-        for d in range(chips):
-            forward(h, d).wait_recv()
-            block = jnp.concatenate([same[h, d], other[h, d]], axis=1)
-            a, b = source(d) + core, source(d) + 1 - core
-            for ref in (high, low):
-                total += lax.dot_general(
-                    block, jnp.concatenate([ref[a], ref[b]], axis=1),
-                    (((1,), (1,)), ((), ())), preferred_element_type=F32,
-                )
+        total = None
+        for held, side in ((same, core), (other, 1 - core)):
+            for i in range(0, chips, 2):
+                pair = (i, i + 1)
+                if held is other:
+                    for d in pair:
+                        forward(h, d).wait_recv()
+                block = jnp.concatenate([held[h, d] for d in pair], axis=1)
+                value = wide(block, [source(d) + side for d in pair], 1)
+                total = value if total is None else total + value
         dual[scenarios(h), :] = jnp.maximum(
             dual[scenarios(h), :] + STEP * (bound[scenarios(h), :] - total), 0.0
         )
@@ -216,7 +225,7 @@
     size = tile_values.shape[1]
     count = primal_start.shape[1]
     blocks = n * primal_start.shape[0] // size
-    assert blocks == n and n % 2 == 0
+    assert blocks == n and n % 4 == 0
     rows = dual_start.shape[0]
     row_blocks = rows // size
     high, low = dense(tile_values, tile_row, tile_col, blocks, row_blocks)

time: 64.3 us -> 60.1 us (0.935)
  Pallas kernels: 58.8 us -> 55 us
    pallas_call x1, Pallas kernels: 57.1 us -> 53.4 us  [body(): pl.pallas_call(functools.partial(iterate_kernel, n, halves), out_shape=(j...]
where the time goes in v1:
time: 60.1 us; the launch traced here: 59.9 us
  Pallas kernels  55 us (92%)
  local copies, waits for them, and re-layouts  4.21 us (7%)
  between operations  0.71 us (1%)
    pallas_call x1, Pallas kernels, body(): pl.pallas_call(functools.partial(iterate_kernel, n, halves), out_shape=(j...  53.4 us
    unnamed x18, local copies, waits for them, and re-layouts  4.21 us
    pallas_call x1, Pallas kernels, dense(): pl.pallas_call(functools.partial(dense_kernel, chunks, row_blocks), out_s...  1.65 us

profile of v1, /device:TPU:0, one launch (start us, length us, event | category | flops | bytes accessed | tf_op | source)
XLA Modules:
  0.0 59.9 jit_solution(17693722445357145222)
XLA Ops:
  0.6 0.0 copy-start.7
  0.6 0.0 copy-start
  0.7 1.6 %copy-done = bf16[64,128,128]{2,1,0:T(8,128)(2,1)S(1)} copy-done((bf16[64,128,128]{2,1,0:T(8,128)(2,1)S(1)}, bf16[64,128,128]{2,1,0:T(8,128)(2,1)}, u32[]{:S(2)}) %copy-start) | copy-done | bytes 2097176
  2.2 0.0 copy-start.5
  2.2 0.7 %copy-done.5 = s32[64]{0:T(128)S(1)} copy-done((s32[64]{0:T(128)S(1)}, s32[64]{0:T(128)}, u32[]{:S(2)}) %copy-start.5) | copy-done | bytes 280
  2.9 0.0 copy-start.6
  2.9 0.7 %copy-done.6 = s32[64]{0:T(128)S(1)} copy-done((s32[64]{0:T(128)S(1)}, s32[64]{0:T(128)}, u32[]{:S(2)}) %copy-start.6) | copy-done | bytes 280
  3.6 0.0 copy-start.1
  3.6 0.0 copy-start.2
  3.6 0.0 copy-start.3
  3.6 0.0 copy-start.4
  3.6 1.6 %shard_map.95 = (bf16[32,128,128]{2,1,0:T(8,128)(2,1)S(1)}, bf16[32,128,128]{2,1,0:T(8,128)(2,1)S(1)}) custom-call(s32[64]{0:T(128)S(1)} %copy-done.5, s32[64]{0:T(128)S(1)} %copy-done.6, bf16[64,128,128]{2,1,0:T(8,128)(2,1)S(1)} %copy-done), custom_call_target="tpu_custom_call" | custom-call | tf_op jit(solution)/shard_map/pallas_call | solution.py:51
  5.2 0.0 copy-done.7
  5.2 0.0 copy-done.1
  5.2 0.0 copy-done.2
  5.2 0.0 copy-done.3
  5.3 0.0 copy-done.4
  5.3 53.4 %shard_map.96 = (f32[128,128]{1,0:T(8,128)S(1)}, f32[256,128]{1,0:T(8,128)S(1)}) custom-call(bf16[16,256,128]{2,1,0:T(8,128)(2,1)S(1)} %bitcast.3, bf16[16,256,128]{2,1,0:T(8,128)(2,1)S(1)} %bitcast.4, f32[128,128]{1,0:T(8,128)S(1)} %copy-done.3, f32[128,128]{1,0:T(8,128)S(1)} %copy-done.4, f32[1,128]{1,0:T(1,128)S(1)} %bitcast.5, f32[256,128]{1,0:T(8,128)S(1)} %copy-done.1, ...), custom_call_target="tpu_custom_call" | custom-call | tf_op jit(solution)/shard_map/pallas_call | solution.py:240
  58.7 0.6 %copy.12 = f32[128,128]{1,0:T(8,128)} copy(f32[128,128]{1,0:T(8,128)S(1)} %get-tuple-element.8) | data formatting | bytes 131072
  59.3 0.7 %copy.13 = f32[256,128]{1,0:T(8,128)} copy(f32[256,128]{1,0:T(8,128)S(1)} %get-tuple-element.9) | data formatting | bytes 262144
Async XLA Ops:
  0.6 4.6 %copy-start.7 = (f32[128]{0:T(128)S(1)}, f32[128]{0:T(128)}, u32[]{:S(2)}) copy-start(f32[128]{0:T(128)} %param.13) | copy-start | bytes 1540
  0.6 1.6 %copy-start = (bf16[64,128,128]{2,1,0:T(8,128)(2,1)S(1)}, bf16[64,128,128]{2,1,0:T(8,128)(2,1)}, u32[]{:S(2)}) copy-start(bf16[64,128,128]{2,1,0:T(8,128)(2,1)} %tiles.1) | copy-start | bytes 6291460
  2.2 0.7 %copy-start.5 = (s32[64]{0:T(128)S(1)}, s32[64]{0:T(128)}, u32[]{:S(2)}) copy-start(s32[64]{0:T(128)} %rows.1) | copy-start | bytes 772
  2.9 0.7 %copy-start.6 = (s32[64]{0:T(128)S(1)}, s32[64]{0:T(128)}, u32[]{:S(2)}) copy-start(s32[64]{0:T(128)} %cols.1) | copy-start | bytes 772
  3.6 1.7 %copy-start.1 = (f32[256,128]{1,0:T(8,128)S(1)}, f32[256,128]{1,0:T(8,128)}, u32[]{:S(2)}) copy-start(f32[256,128]{1,0:T(8,128)} %dual_start.1) | copy-start | bytes 393220
  3.6 1.7 %copy-start.2 = (f32[256,128]{1,0:T(8,128)S(1)}, f32[256,128]{1,0:T(8,128)}, u32[]{:S(2)}) copy-start(f32[256,128]{1,0:T(8,128)} %row_bound.1) | copy-start | bytes 393220
  3.6 1.7 %copy-start.3 = (f32[128,128]{1,0:T(8,128)S(1)}, f32[128,128]{1,0:T(8,128)}, u32[]{:S(2)}) copy-start(f32[128,128]{1,0:T(8,128)} %primal_start.1) | copy-start | bytes 196612
  3.6 1.7 %copy-start.4 = (f32[128,128]{1,0:T(8,128)S(1)}, f32[128,128]{1,0:T(8,128)}, u32[]{:S(2)}) copy-start(f32[128,128]{1,0:T(8,128)} %objective.1) | copy-start | bytes 196612

commit v2 on v1

--- a/solution.py
+++ b/solution.py
@@ -14,24 +14,12 @@
 BF16 = jnp.bfloat16
 
 
-def dense_kernel(chunks, row_blocks, rows, cols, tiles, high, low, total, held, arrived):
-    group = held.shape[0] // chunks
-
-    def copy(k):
-        part = pl.ds(k * group, group)
-        return pltpu.make_async_copy(tiles.at[part], held.at[part], arrived.at[k])
-
-    for k in range(chunks):
-        copy(k).start()
+def dense_kernel(places, tiles, high, low, total):
     total[...] = jnp.zeros_like(total)
-    for k in range(chunks):
-        copy(k).wait()
-
-        @pl.loop(0, group, unroll=min(group, 8))
-        def _(i):
-            t = k * group + i
-            at = cols[t] * row_blocks + rows[t]
-            total[at] += held[t].astype(F32)
+
+    @pl.loop(0, tiles.shape[0], unroll=8)
+    def _(t):
+        total[places[t]] += tiles[t].astype(F32)
 
     @pl.loop(0, total.shape[0], unroll=4)
     def _(b):
@@ -43,23 +31,18 @@
 
 def dense(tile_values, tile_row, tile_col, blocks, row_blocks):
     tiles, size, _ = tile_values.shape
-    chunks = 8
     shape = jax.ShapeDtypeStruct((blocks * row_blocks, size, size), BF16)
     smem = pl.BlockSpec(memory_space=pltpu.SMEM)
     vmem = pl.BlockSpec(memory_space=pltpu.VMEM)
-    room = size * size * (4 * blocks * row_blocks + 2 * tiles + 4 * blocks * row_blocks)
+    room = size * size * (8 * blocks * row_blocks + 2 * tiles)
     return pl.pallas_call(
-        functools.partial(dense_kernel, chunks, row_blocks),
+        dense_kernel,
         out_shape=(shape, shape),
-        in_specs=[smem, smem, pl.BlockSpec(memory_space=pltpu.HBM)],
+        in_specs=[smem, vmem],
         out_specs=(vmem, vmem),
-        scratch_shapes=[
-            pltpu.VMEM((blocks * row_blocks, size, size), F32),
-            pltpu.VMEM((tiles, size, size), BF16),
-            pltpu.SemaphoreType.DMA((chunks,)),
-        ],
+        scratch_shapes=[pltpu.VMEM((blocks * row_blocks, size, size), F32)],
         compiler_params=pltpu.CompilerParams(vmem_limit_bytes=room + (4 << 20)),
-    )(tile_row, tile_col, tile_values)
+    )(tile_col * row_blocks + tile_row, tile_values)
 
 
 def iterate_kernel(

time: 60.1 us -> 59.2 us (0.985)
  local copies, waits for them, and re-layouts: 4.21 us -> 2.9 us
  other arithmetic: 0 us -> 0.68 us
    unnamed x18 -> x14, local copies, waits for them, and re-layouts: 4.21 us -> 2.9 us
    add x0 -> x1, other arithmetic: none -> 0.68 us  [dense(): tile_col * row_blocks + tile_row]
where the time goes in v2:
time: 59.2 us; the launch traced here: 59 us
  Pallas kernels  54.8 us (93%)
  local copies, waits for them, and re-layouts  2.9 us (5%)
  between operations  0.7 us (1%)
  other arithmetic  0.68 us (1%)
    pallas_call x1, Pallas kernels, body(): pl.pallas_call(functools.partial(iterate_kernel, n, halves), out_shape=(j...  53.4 us
    unnamed x14, local copies, waits for them, and re-layouts  2.9 us
    pallas_call x1, Pallas kernels, dense(): pl.pallas_call(dense_kernel, out_shape=(shape, shape), in_specs=[smem, vm...  1.37 us

profile of v2, /device:TPU:0, one launch (start us, length us, event | category | flops | bytes accessed | tf_op | source)
XLA Modules:
  0.0 59.0 jit_solution(6682875144262277590)
XLA Ops:
  0.6 0.0 copy-start.5
  0.6 0.7 %multiply_add_fusion.places = s32[64]{0:T(128)S(1)} fusion(s32[64]{0:T(128)} %param.9, s32[64]{0:T(128)} %param.10), kind=kLoop, calls=%fused_computation | loop fusion | flops 128 | bytes 768 | tf_op jit(solution)/shard_map/add | solution.py:45
  1.3 0.0 copy-start
  1.3 1.6 %copy-done = bf16[64,128,128]{2,1,0:T(8,128)(2,1)S(1)} copy-done((bf16[64,128,128]{2,1,0:T(8,128)(2,1)S(1)}, bf16[64,128,128]{2,1,0:T(8,128)(2,1)}, u32[]{:S(2)}) %copy-start) | copy-done | bytes 2097176
  2.9 0.0 copy-start.1
  2.9 0.0 copy-start.2
  2.9 0.0 copy-start.3
  2.9 0.0 copy-start.4
  2.9 1.4 %shard_map.95 = (bf16[32,128,128]{2,1,0:T(8,128)(2,1)S(1)}, bf16[32,128,128]{2,1,0:T(8,128)(2,1)S(1)}) custom-call(s32[64]{0:T(128)S(1)} %multiply_add_fusion.places, bf16[64,128,128]{2,1,0:T(8,128)(2,1)S(1)} %copy-done), custom_call_target="tpu_custom_call" | custom-call | tf_op jit(solution)/shard_map/pallas_call | solution.py:38
  4.3 0.0 copy-done.5
  4.3 0.0 copy-done.1
  4.3 0.0 copy-done.2
  4.3 0.0 copy-done.3
  4.3 0.0 copy-done.4
  4.4 53.4 %shard_map.96 = (f32[128,128]{1,0:T(8,128)S(1)}, f32[256,128]{1,0:T(8,128)S(1)}) custom-call(bf16[16,256,128]{2,1,0:T(8,128)(2,1)S(1)} %bitcast.3, bf16[16,256,128]{2,1,0:T(8,128)(2,1)S(1)} %bitcast.4, f32[128,128]{1,0:T(8,128)S(1)} %copy-done.3, f32[128,128]{1,0:T(8,128)S(1)} %copy-done.4, f32[1,128]{1,0:T(1,128)S(1)} %bitcast.5, f32[256,128]{1,0:T(8,128)S(1)} %copy-done.1, ...), custom_call_target="tpu_custom_call" | custom-call | tf_op jit(solution)/shard_map/pallas_call | solution.py:223
  57.7 0.6 %copy.12 = f32[128,128]{1,0:T(8,128)} copy(f32[128,128]{1,0:T(8,128)S(1)} %get-tuple-element.8) | data formatting | bytes 131072
  58.4 0.7 %copy.13 = f32[256,128]{1,0:T(8,128)} copy(f32[256,128]{1,0:T(8,128)S(1)} %get-tuple-element.9) | data formatting | bytes 262144
Async XLA Ops:
  0.6 3.7 %copy-start.5 = (f32[128]{0:T(128)S(1)}, f32[128]{0:T(128)}, u32[]{:S(2)}) copy-start(f32[128]{0:T(128)} %param.13) | copy-start | bytes 1540
  1.3 1.6 %copy-start = (bf16[64,128,128]{2,1,0:T(8,128)(2,1)S(1)}, bf16[64,128,128]{2,1,0:T(8,128)(2,1)}, u32[]{:S(2)}) copy-start(bf16[64,128,128]{2,1,0:T(8,128)(2,1)} %tiles.1) | copy-start | bytes 6291460
  2.9 1.4 %copy-start.1 = (f32[256,128]{1,0:T(8,128)S(1)}, f32[256,128]{1,0:T(8,128)}, u32[]{:S(2)}) copy-start(f32[256,128]{1,0:T(8,128)} %dual_start.1) | copy-start | bytes 393220
  2.9 1.4 %copy-start.2 = (f32[256,128]{1,0:T(8,128)S(1)}, f32[256,128]{1,0:T(8,128)}, u32[]{:S(2)}) copy-start(f32[256,128]{1,0:T(8,128)} %row_bound.1) | copy-start | bytes 393220
  2.9 1.4 %copy-start.3 = (f32[128,128]{1,0:T(8,128)S(1)}, f32[128,128]{1,0:T(8,128)}, u32[]{:S(2)}) copy-start(f32[128,128]{1,0:T(8,128)} %primal_start.1) | copy-start | bytes 196612
  2.9 1.4 %copy-start.4 = (f32[128,128]{1,0:T(8,128)S(1)}, f32[128,128]{1,0:T(8,128)}, u32[]{:S(2)}) copy-start(f32[128,128]{1,0:T(8,128)} %objective.1) | copy-start | bytes 196612
